TPU v7x, 128 devices: a whole 4x4x4 slice. The times are simulated.
128 devices in a mesh: grp: 4 (over z), dev: 32 (over y, x, core).
Axes of the slice: x: 4, y: 4, z: 4, core: 2. Of those that a mesh axis runs over, the one named last changes fastest.
Arguments:
- hidden_rows: bfloat16 [1024, 7168], P(('grp', 'dev')), may hold values from -6 to 6
- queries: bfloat16 [1024, 128, 576], P(('grp', 'dev')), may hold values from -320 to 320
- kv_cache: bfloat16 [1024, 512, 576], P(('grp', 'dev')), may hold values from -4 to 4
- cache_lengths: int32 [1024], P(('grp', 'dev')), may hold values from 2 to 512, as said below
- value_lift: bfloat16 [128, 512, 128], P('dev'), may hold values from -0.25 to 0.25
- out_weight: bfloat16 [128, 128, 7168], P('dev'), may hold values from -0.046875 to 0.046875
- expert_ids: int32 [1024, 8], P(('grp', 'dev')), may hold values from 0 to 31, all different within a row; in each aligned block of 4 rows (0 to 3, 4 to 7, ...) at most 2 rows name the same one
- weight_codes: int32 [1024, 8], P(('grp', 'dev')), may hold values from 1 to 255
- w_gate: bfloat16 [32, 7168, 1024], P('dev', None, 'grp'), may hold values from -0.0625 to 0.0625
- w_up: bfloat16 [32, 7168, 1024], P('dev', None, 'grp'), may hold values from -0.0625 to 0.0625
- w_down: bfloat16 [32, 1024, 7168], P('dev', 'grp'), may hold values from -0.1875 to 0.1875
Outputs:
- layer_out: bfloat16 [1024, 7168], P(('grp', 'dev'))
Inputs may be any that keep to these rules, and one draw needn't show every extreme that they name: `expert_ids`: each row names 8 different experts; in each aligned block of 4 rows no expert is named by more than 2 rows, and in some block one expert is named by exactly 2. `cache_lengths`: some request has exactly 512 live positions.
All inputs are finite; a program needn't handle non-finite values.
Results may differ from a plain program's by a relative error of at most 0.012.
Values may be sent and summed in bfloat16 or wider, within the bound.
No kernel may reach another device: no remote copies, remote signals or barrier semaphores. Data moves between devices by JAX's collectives and lax.ppermute only.
A program may use at most 128 MiB of HBM per device.

v0:
```python
import jax
import jax.numpy as jnp
from jax import lax
from jax.experimental import pallas as pl
from jax.experimental.pallas import tpu as pltpu
from jax.sharding import PartitionSpec as P


LATENT = 512
SCALE = 192.0 ** (-0.5)
ALL = ("grp", "dev")
BF = jnp.bfloat16
F32 = jnp.float32


def place(i):
    return [i // 32, (i // 8) % 4, (i // 2) % 4, i % 2]


def number(at):
    return ((at[0] * 4 + at[1]) * 4 + at[2]) * 2 + at[3]


def core_pairs():
    return [(i, i ^ 1) for i in range(128)]


def ring_pairs(axis, step):
    pairs = []
    for i in range(128):
        at = place(i)
        flip = (1, 3) if at[3] == 0 else (3, 1)
        at[axis] ^= flip[step]
        pairs.append((i, number(at)))
    return pairs


def ring_next(axis, hops=1):
    pairs = []
    for i in range(128):
        at = place(i)
        at[axis] = (at[axis] + (hops if at[3] == 0 else 4 - hops)) % 4
        pairs.append((i, number(at)))
    return pairs


Z, Y, X = 0, 1, 2


def swap(value, axis, step):
    return lax.ppermute(value, ALL, ring_pairs(axis, step))


def onward(value, axis, hops=1):
    return lax.ppermute(value, ALL, ring_next(axis, hops))


def other_core(value):
    return lax.ppermute(value, ALL, core_pairs())


PER_STEP = 2
PARTS = 1


def attend_kernel(first, length_ref, q_ref, kv_ref, out_ref):
    for j in range(PER_STEP):
        kv = kv_ref[j]
        logits = lax.dot_general(
            q_ref[j], kv, (((0,), (0,)), ((), ())), preferred_element_type=F32
        ) * SCALE
        live = lax.broadcasted_iota(jnp.int32, logits.shape, 1) < length_ref[
            first + pl.program_id(0) * PER_STEP + j
        ]
        logits = jnp.where(live, logits, -jnp.inf)
        exponent = jnp.exp(logits - jnp.max(logits, axis=1, keepdims=True))
        soft = (exponent / jnp.sum(exponent, axis=1, keepdims=True)).astype(BF)
        result = lax.dot_general(
            soft, kv[:LATENT], (((1,), (1,)), ((), ())), preferred_element_type=F32
        )
        out_ref[:, j] = result.astype(BF).reshape(out_ref.shape[0], out_ref.shape[2], LATENT)


def attend(queries, kv_cache, cache_lengths, first, rows):
    _, heads, depth = queries.shape
    live = kv_cache.shape[1]
    skip = first // PER_STEP
    return pl.pallas_call(
        lambda *refs: attend_kernel(first, *refs),
        grid_spec=pltpu.PrefetchScalarGridSpec(
            num_scalar_prefetch=1,
            grid=(rows // PER_STEP,),
            in_specs=[
                pl.BlockSpec((PER_STEP, depth, heads), lambda i, n: (i + skip, 0, 0)),
                pl.BlockSpec((PER_STEP, depth, live), lambda i, n: (i + skip, 0, 0)),
            ],
            out_specs=pl.BlockSpec((16, PER_STEP, heads // 16, LATENT), lambda i, n: (0, i, 0, 0)),
        ),
        out_shape=jax.ShapeDtypeStruct((16, rows, heads // 16, LATENT), BF),
        name="attend",
    )(cache_lengths, jnp.swapaxes(queries, 1, 2), jnp.swapaxes(kv_cache, 1, 2))


def project_kernel(steps, left_in, right_in, own_ref, other_ref, *outs):
    depth = own_ref.shape[0]

    def run(rows_ref, keep_ref, send_ref):
        result = jnp.dot(rows_ref[:, :depth], own_ref[...], preferred_element_type=F32)
        result += jnp.dot(rows_ref[:, depth:], other_ref[...], preferred_element_type=F32)
        half = result.shape[0] // 2
        keep_ref[...] = result[:half].astype(BF)
        send_ref[...] = result[half:].astype(BF)

    @pl.when(pl.program_id(0) < steps)
    def _():
        run(left_in, *outs[:2])

    @pl.when(pl.program_id(0) >= steps)
    def _():
        run(right_in, *outs[2:])


def project(left_in, right_in, own, other):
    rows, depth = left_in.shape
    width = own.shape[1]
    block = 1792
    steps = width // 2 // block
    whole = pl.BlockSpec((rows, depth), lambda i: (0, 0))
    matrix = pl.BlockSpec((depth // 2, block), lambda i: (0, i))
    shape = jax.ShapeDtypeStruct((rows // 2, width // 2), BF)
    left_out = pl.BlockSpec((rows // 2, block), lambda i: (0, jnp.minimum(i, steps - 1)))
    right_out = pl.BlockSpec((rows // 2, block), lambda i: (0, jnp.maximum(i - steps, 0)))
    return pl.pallas_call(
        lambda *refs: project_kernel(steps, *refs),
        grid=(2 * steps,),
        in_specs=[whole, whole, matrix, matrix],
        out_specs=[left_out, left_out, right_out, right_out],
        out_shape=[shape] * 4,
        name="project",
    )(left_in, right_in, own, other)


BLOCK = 1024
AHEAD = 3


def experts_kernel(
    number_ref, xa, xb, gate_own, up_own, gate_other, up_other, down_own, down_other,
    out_a, out_b, rows_ref, into, back, acc, hidden, row_sems, into_sems, back_sems,
):
    rows = xa.shape[0]
    steps, _, _, units = into.shape
    width = steps * BLOCK
    inward = (gate_own, up_own, gate_other, up_other)
    outward = (down_own, down_other)

    def span(step):
        return pl.ds(pl.multiple_of(step * BLOCK, BLOCK), BLOCK)

    def into_copies(step):
        return [
            pltpu.make_async_copy(m.at[0, span(step)], into.at[step, at], into_sems.at[step, at])
            for at, m in enumerate(inward)
        ]

    def back_copies(step):
        return [
            pltpu.make_async_copy(
                m.at[0, :, span(step)], back.at[step, at], back_sems.at[step, at]
            )
            for at, m in enumerate(outward)
        ]

    def start(copies):
        for copy in copies:
            copy.start()

    def wait(copies):
        for copy in copies:
            copy.wait()

    row_copies = [
        pltpu.make_async_copy(xa, rows_ref.at[:rows], row_sems.at[0]),
        pltpu.make_async_copy(xb, rows_ref.at[rows:], row_sems.at[1]),
    ]
    start(row_copies)
    for step in range(AHEAD):
        start(into_copies(step))
    acc[...] = jnp.zeros_like(acc)
    wait(row_copies)

    def inward_step(step, carry):
        @pl.when(step + AHEAD < steps)
        def _():
            start(into_copies(step + AHEAD))

        @pl.when(step + AHEAD >= steps)
        def _():
            start(back_copies(step + AHEAD - steps))

        wait(into_copies(step))
        block = rows_ref[:, span(step)]
        for at in range(4):
            acc[at] += jnp.dot(block, into[step, at], preferred_element_type=F32)
        return carry

    lax.fori_loop(0, steps, inward_step, 0)
    table = rows_ref[:, width:].astype(F32)
    ids, codes = table[:, :8], table[:, 8:16]
    weights = 2.5 * codes / jnp.sum(codes, axis=1, keepdims=True)
    for at in range(2):
        gate, up = acc[2 * at], acc[2 * at + 1]
        named = ids == number_ref[at].astype(F32)
        share = jnp.sum(jnp.where(named, weights, 0.0), axis=1, keepdims=True)
        value = gate / (1.0 + jnp.exp(-gate)) * up * share
        hidden[:, at * units : (at + 1) * units] = value.astype(BF)

    def outward_step(step, carry):
        @pl.when(step + AHEAD < steps)
        def _():
            start(back_copies(step + AHEAD))

        wait(back_copies(step))
        result = jnp.dot(hidden[:, :units], back[step, 0], preferred_element_type=F32)
        result += jnp.dot(hidden[:, units:], back[step, 1], preferred_element_type=F32)
        out_a[:, span(step)] = result[:rows].astype(BF)
        out_b[:, span(step)] = result[rows:].astype(BF)
        return carry

    lax.fori_loop(0, steps, outward_step, 0)


def experts(numbers, xa, xb, weights, width):
    rows = xa.shape[0]
    units = weights[0].shape[2]
    steps = width // BLOCK
    shape = jax.ShapeDtypeStruct((rows, width), BF)
    vmem = pl.BlockSpec(memory_space=pltpu.VMEM)
    far = pl.BlockSpec(memory_space=pl.ANY)
    return pl.pallas_call(
        experts_kernel,
        in_specs=[pl.BlockSpec(memory_space=pltpu.SMEM)] + [far] * 8,
        out_specs=[vmem, vmem],
        out_shape=[shape, shape],
        scratch_shapes=[
            pltpu.VMEM((2 * rows, xa.shape[1]), BF),
            pltpu.VMEM((steps, 4, BLOCK, units), BF),
            pltpu.VMEM((steps, 2, units, BLOCK), BF),
            pltpu.VMEM((4, 2 * rows, units), F32),
            pltpu.VMEM((2 * rows, 2 * units), BF),
            pltpu.SemaphoreType.DMA((2,)),
            pltpu.SemaphoreType.DMA((steps, 4)),
            pltpu.SemaphoreType.DMA((steps, 2)),
        ],
        compiler_params=pltpu.CompilerParams(vmem_limit_bytes=32 << 20),
        name="experts",
    )(numbers, xa, xb, *weights)


def ring_offset(bits, core):
    low, high = bits % 2, bits // 2
    first = jnp.where(core == 0, 1, 3)
    second = jnp.where(core == 0, 3, 1)
    return (low * first) ^ (high * second)


def plane_order(rows, here, core, y_first):
    count = rows // 16
    at = jnp.arange(rows, dtype=jnp.int32)
    block = at // count
    major, minor = block // 4, block % 4
    y = (here // 4) ^ ring_offset(major if y_first else minor, core)
    x = (here % 4) ^ ring_offset(minor if y_first else major, core)
    part = count // PARTS
    request = at % count
    source = (request // part) * (16 * part) + (y * 4 + x) * part + request % part
    return (source[:, None] == jnp.arange(rows, dtype=jnp.int32)[None, :]).astype(BF)


def halves(value):
    half = value.shape[0] // 2
    return value[:half], value[half:]


def add(one, two):
    return (one.astype(F32) + two.astype(F32)).astype(BF)


def fold(value, axis, step):
    keep, send = halves(value)
    got = swap(send, axis, step)
    return (keep.astype(F32) + got.astype(F32)).astype(BF)


def grow(value, axis, step):
    return jnp.concatenate([value, swap(value, axis, step)], axis=0)


def run_rows(
    hidden_rows,
    queries,
    kv_cache,
    cache_lengths,
    value_lift,
    out_weight,
    expert_ids,
    weight_codes,
    w_gate,
    w_up,
    w_down,
):
    device = lax.axis_index("dev")
    core = device % 2
    here = device // 2
    rows, width = hidden_rows.shape

    swapped = []
    for matrix in (value_lift, out_weight, w_gate, w_up, w_down):
        swapped.append(other_core(matrix))
    lift_other, out_other, gate_other, up_other, down_other = swapped

    same_core = [[c + 2 * i for i in range(16)] for c in range(2)]
    moved = []
    for at in range(PARTS):
        heads_out = attend(queries, kv_cache, cache_lengths, at * (rows // PARTS), rows // PARTS)
        arrived = lax.all_to_all(
            heads_out, "dev", split_axis=0, concat_axis=0, tiled=True,
            axis_index_groups=same_core,
        )
        moved.append(arrived.reshape(-1, arrived.shape[2], LATENT))
    all_rows = 16 * rows

    def lifted(part, lift):
        return jnp.einsum("rhl,hlv->rhv", part, lift, preferred_element_type=F32).astype(BF)

    def head_pair(arrived):
        own = lax.dynamic_slice_in_dim(arrived, 4 * core, 4, 1)
        other = lax.dynamic_slice_in_dim(arrived, 4 * (1 - core), 4, 1)
        return jnp.concatenate(
            [lifted(own, value_lift), lifted(other, lift_other)], axis=1
        ).reshape(all_rows // PARTS, -1)

    head_values = jnp.concatenate([head_pair(arrived) for arrived in moved], axis=0)

    def ordered(y_first):
        order = plane_order(all_rows, here, core, y_first)
        return jnp.dot(order, head_values, preferred_element_type=F32).astype(BF)

    left_keep, left_send, right_keep, right_send = project(
        ordered(True),
        ordered(False),
        out_weight.reshape(-1, width),
        out_other.reshape(-1, width),
    )
    left = add(left_keep, swap(left_send, Y, 1))
    right = add(right_keep, swap(right_send, X, 1))
    for axis_left, axis_right, step in ((Y, X, 0), (X, Y, 1), (X, Y, 0)):
        left = fold(left, axis_left, step)
        right = fold(right, axis_right, step)
    attention = jnp.concatenate([left, right], axis=1).astype(F32)
    residual = hidden_rows.astype(F32) + attention
    normed = (
        residual * lax.rsqrt(jnp.mean(residual * residual, axis=1, keepdims=True) + 1e-06)
    ).astype(BF)

    routing = jnp.concatenate([expert_ids, weight_codes], axis=1).astype(BF)
    routing = jnp.pad(routing, ((0, 0), (0, 128 - routing.shape[1])))
    mine = jnp.concatenate([normed, routing], axis=1)
    from_one, from_two, from_three = [onward(mine, Z, hops) for hops in (1, 2, 3)]
    first = jnp.concatenate([mine, from_one], axis=0)
    second = jnp.concatenate([from_two, from_three], axis=0)
    for step in range(2):
        first = grow(first, X, step)
        second = grow(second, Y, step)

    numbers = jnp.stack([device, device ^ 1]).astype(jnp.int32)
    weights = (w_gate, w_up, gate_other, up_other, w_down, down_other)

    def both(pair, hops):
        moved_on = []
        for at, axis in enumerate((Y, X)):
            moved_on.append(onward(pair[at], axis, hops))
        return moved_on

    held = [(first, second)]
    held.append(both(held[0], 1))
    from_ahead = both(held[0], 3)
    held.append(both(held[1], 1))
    held.append(from_ahead)
    done = []
    for hop in range(4):
        done.append(experts(numbers, *held[hop], weights, width))
    near = both(done[1], 3)
    far = both(done[2], 1)
    far = [add(done[3][at], far[at]) for at in range(2)]
    far = both(far, 1)
    one, two = [
        (done[0][at].astype(F32) + near[at].astype(F32) + far[at].astype(F32)).astype(BF)
        for at in range(2)
    ]
    for step in (1, 0):
        one = fold(one, X, step)
        two = fold(two, Y, step)
    keep, to_one = halves(one)
    to_two, to_three = halves(two)
    combined = keep.astype(F32)
    for part, hops in ((to_one, 3), (to_two, 2), (to_three, 1)):
        combined += onward(part, Z, hops).astype(F32)
    return (residual + combined).astype(BF)


def solution(mesh):
    both = P(ALL, None)
    in_specs = (
        both,
        P(ALL, None, None),
        P(ALL, None, None),
        P(ALL),
        P("dev", None, None),
        P("dev", None, None),
        both,
        both,
        P("dev", None, "grp"),
        P("dev", None, "grp"),
        P("dev", "grp", None),
    )
    return jax.shard_map(run_rows, mesh=mesh, in_specs=in_specs, out_specs=both, check_vma=False)
```

profile of v0, /device:TPU:0, one launch (start us, length us, event | category | flops | bytes accessed | tf_op | source)
XLA Modules:
  0.0 249.7 jit_solution(15403542785147127578)
XLA Ops:
  0.0 8.0 %attend.1 = bf16[16,8,8,512]{3,2,1,0:T(8,128)(2,1)} custom-call(s32[8]{0:T(128)} %refs_0_.1, bf16[8,576,128]{2,1,0:T(8,128)(2,1)} %bitcast.21, bf16[8,576,512]{2,1,0:T(8,128)(2,1)} %bitcast.17), custom_call_target="tpu_custom_call" | custom-call | tf_op jit(solution)/shard_map/attend/pallas_call | solution.py:88
  8.0 7.3 %all-to-all-start = ((bf16[16,8,8,512]{3,2,1,0:T(8,128)(2,1)}), bf16[16,8,8,512]{3,2,1,0:T(8,128)(2,1)S(1)}, u32[]{:S(2)}, u32[]{:S(2)}) async-start(bf16[16,8,8,512]{3,2,1,0:T(8,128)(2,1)} %attend.1), calls=%async_computation | async-start | bytes 2097152 | tf_op jit(solution)/shard_map/all_to_all | solution.py:326
  15.9 18.1 %all-to-all-done = bf16[16,8,8,512]{3,2,1,0:T(8,128)(2,1)S(1)} async-done(((bf16[16,8,8,512]{3,2,1,0:T(8,128)(2,1)}), bf16[16,8,8,512]{3,2,1,0:T(8,128)(2,1)S(1)}, u32[]{:S(2)}, u32[]{:S(2)}) %all-to-all-start) | async-done | bytes 1048608 | tf_op jit(solution)/shard_map/all_to_all | solution.py:326
  37.1 8.0 %project.1 = (bf16[64,3584]{1,0:T(8,128)(2,1)}, bf16[64,3584]{1,0:T(8,128)(2,1)}, bf16[64,3584]{1,0:T(8,128)(2,1)}, bf16[64,3584]{1,0:T(8,128)(2,1)}) custom-call(bf16[128,1024]{1,0:T(8,128)(2,1)} %convolution_convert_fusion.1.refs_0_, bf16[128,1024]{1,0:T(8,128)(2,1)} %convolution_convert_fusion.refs_1_, bf16[512,7168]{1,0:T(8,128)(2,1)} %bitcast.16, ...), custom_call_target="tpu_custom_call" | custom-call | tf_op jit(solution)/shard_map/project/pallas_call | solution.py:133
  47.1 8.0 %collective-permute-done.2 = bf16[64,3584]{1,0:T(8,128)(2,1)S(1)} collective-permute-done((bf16[64,3584]{1,0:T(8,128)(2,1)}, bf16[64,3584]{1,0:T(8,128)(2,1)S(1)}, u32[]{:S(2)}, u32[]{:S(2)}) %collective-permute-start.2) | collective-permute-done | bytes 458784 | tf_op jit(solution)/shard_map/ppermute | solution.py:51
  56.6 5.7 %collective-permute-done.3 = bf16[32,3584]{1,0:T(8,128)(2,1)S(1)} collective-permute-done((bf16[32,3584]{1,0:T(8,128)(2,1)S(1)}, bf16[32,3584]{1,0:T(8,128)(2,1)S(1)}, u32[]{:S(2)}, u32[]{:S(2)}) %collective-permute-start.3) | collective-permute-done | bytes 229408 | tf_op jit(solution)/shard_map/ppermute | solution.py:51
  63.2 2.9 %collective-permute-start.8 = (bf16[16,3584]{1,0:T(8,128)(2,1)S(1)}, bf16[16,3584]{1,0:T(8,128)(2,1)S(1)}, u32[]{:S(2)}, u32[]{:S(2)}) collective-permute-start(bf16[16,3584]{1,0:T(8,128)(2,1)S(1)} %slice.105), channel_id=1, source_target_pairs={{0,24},{1,9},{2,26},{3,11},{4,28},{5,13},{6,30},{7,15},{8,16},{9,1... | collective-permute-start | bytes 344072 | tf_op jit(solution)/shard_map/ppermute | solution.py:51
  66.1 3.0 %collective-permute-done.4 = bf16[16,3584]{1,0:T(8,128)(2,1)S(1)} collective-permute-done((bf16[16,3584]{1,0:T(8,128)(2,1)S(1)}, bf16[16,3584]{1,0:T(8,128)(2,1)S(1)}, u32[]{:S(2)}, u32[]{:S(2)}) %collective-permute-start.4) | collective-permute-done | bytes 114720 | tf_op jit(solution)/shard_map/ppermute | solution.py:51
  70.1 3.4 %collective-permute-done.5 = bf16[8,3584]{1,0:T(8,128)(2,1)S(1)} collective-permute-done((bf16[8,3584]{1,0:T(8,128)(2,1)S(1)}, bf16[8,3584]{1,0:T(8,128)(2,1)S(1)}, u32[]{:S(2)}, u32[]{:S(2)}) %collective-permute-start.5) | collective-permute-done | bytes 57376 | tf_op jit(solution)/shard_map/ppermute | solution.py:51
  74.6 4.0 %collective-permute-start.13 = (bf16[8,7296]{1,0:T(8,128)(2,1)S(1)}, bf16[8,7296]{1,0:T(8,128)(2,1)S(1)}, u32[]{:S(2)}, u32[]{:S(2)}) collective-permute-start(bf16[8,7296]{1,0:T(8,128)(2,1)S(1)} %pad_maximum_fusion.6), channel_id=1, source_target_pairs={{0,64},{1,65},{2,66},{3,67},{4,68},{5,69},{6,70},{7,71},{8,72},{9,... | collective-permute-start | bytes 350216 | tf_op jit(solution)/shard_map/ppermute | solution.py:55
  84.4 3.5 %collective-permute-done.10 = bf16[8,7296]{1,0:T(8,128)(2,1)S(1)} collective-permute-done((bf16[8,7296]{1,0:T(8,128)(2,1)S(1)}, bf16[8,7296]{1,0:T(8,128)(2,1)S(1)}, u32[]{:S(2)}, u32[]{:S(2)}) %collective-permute-start.10) | collective-permute-done | bytes 116768 | tf_op jit(solution)/shard_map/ppermute | solution.py:55
  94.5 2.7 %collective-permute-start.12 = (bf16[32,7296]{1,0:T(8,128)(2,1)S(1)}, bf16[32,7296]{1,0:T(8,128)(2,1)S(1)}, u32[]{:S(2)}, u32[]{:S(2)}) collective-permute-start(bf16[32,7296]{1,0:T(8,128)(2,1)S(1)} %pad_maximum_fusion.1), channel_id=1, source_target_pairs={{0,6},{1,3},{2,4},{3,1},{4,2},{5,7},{6,0},{7,5},{8,14},{9,11},{10,... | collective-permute-start | bytes 1400840 | tf_op jit(solution)/shard_map/ppermute | solution.py:51
  97.3 3.8 %collective-permute-done.16 = bf16[32,7296]{1,0:T(8,128)(2,1)S(1)} collective-permute-done((bf16[32,7296]{1,0:T(8,128)(2,1)S(1)}, bf16[32,7296]{1,0:T(8,128)(2,1)S(1)}, u32[]{:S(2)}, u32[]{:S(2)}) %collective-permute-start.16) | collective-permute-done | bytes 466976 | tf_op jit(solution)/shard_map/ppermute | solution.py:51
  102.7 5.7 %collective-permute-done.12 = bf16[32,7296]{1,0:T(8,128)(2,1)S(1)} collective-permute-done((bf16[32,7296]{1,0:T(8,128)(2,1)S(1)}, bf16[32,7296]{1,0:T(8,128)(2,1)S(1)}, u32[]{:S(2)}, u32[]{:S(2)}) %collective-permute-start.12) | collective-permute-done | bytes 466976 | tf_op jit(solution)/shard_map/ppermute | solution.py:51
  108.5 7.4 %collective-permute-done.21.xb = bf16[64,7296]{1,0:T(8,128)(2,1)S(1)} collective-permute-done((bf16[64,7296]{1,0:T(8,128)(2,1)S(1)}, bf16[64,7296]{1,0:T(8,128)(2,1)S(1)}, u32[]{:S(2)}, u32[]{:S(2)}) %collective-permute-start.21) | collective-permute-done | bytes 933920 | tf_op jit(solution)/shard_map/ppermute | solution.py:55
  116.2 10.1 %collective-permute-done.20.xa = bf16[64,7296]{1,0:T(8,128)(2,1)} collective-permute-done((bf16[64,7296]{1,0:T(8,128)(2,1)S(1)}, bf16[64,7296]{1,0:T(8,128)(2,1)}, u32[]{:S(2)}, u32[]{:S(2)}) %collective-permute-start.20) | collective-permute-done | bytes 933920 | tf_op jit(solution)/shard_map/ppermute | solution.py:55
  126.3 4.5 %collective-permute-start.24 = (bf16[64,7296]{1,0:T(8,128)(2,1)S(1)}, bf16[64,7296]{1,0:T(8,128)(2,1)S(1)}, u32[]{:S(2)}, u32[]{:S(2)}) collective-permute-start(bf16[64,7296]{1,0:T(8,128)(2,1)S(1)} %constant_dynamic-update-slice_fusion.xb), channel_id=1, source_target_pairs={{0,6},{1,3},{2,0},{3,5},{4,2},{5,7},{6,4},{7,1},{8,14},{9,11},{10,... | collective-permute-start | bytes 2801672 | tf_op jit(solution)/shard_map/ppermute | solution.py:55
  130.8 3.2 %collective-permute-start.23 = (bf16[64,7296]{1,0:T(8,128)(2,1)S(1)}, bf16[64,7296]{1,0:T(8,128)(2,1)S(1)}, u32[]{:S(2)}, u32[]{:S(2)}) collective-permute-start(bf16[64,7296]{1,0:T(8,128)(2,1)S(1)} %pad_maximum_fusion.xa), channel_id=1, source_target_pairs={{0,24},{1,9},{2,26},{3,11},{4,28},{5,13},{6,30},{7,15},{8,0},{9,17... | collective-permute-start | bytes 2801672 | tf_op jit(solution)/shard_map/ppermute | solution.py:55
  134.2 6.2 %collective-permute-done.26.xb = bf16[64,7296]{1,0:T(8,128)(2,1)} collective-permute-done((bf16[64,7296]{1,0:T(8,128)(2,1)S(1)}, bf16[64,7296]{1,0:T(8,128)(2,1)}, u32[]{:S(2)}, u32[]{:S(2)}) %collective-permute-start.26) | collective-permute-done | bytes 933920 | tf_op jit(solution)/shard_map/ppermute | solution.py:55
  140.3 3.0 %collective-permute-done.25.xa = bf16[64,7296]{1,0:T(8,128)(2,1)} collective-permute-done((bf16[64,7296]{1,0:T(8,128)(2,1)}, bf16[64,7296]{1,0:T(8,128)(2,1)}, u32[]{:S(2)}, u32[]{:S(2)}) %collective-permute-start.25) | collective-permute-done | bytes 933920 | tf_op jit(solution)/shard_map/ppermute | solution.py:55
  143.4 11.1 %experts.7 = (bf16[64,7168]{1,0:T(8,128)(2,1)S(1)}, bf16[64,7168]{1,0:T(8,128)(2,1)S(1)}) custom-call(s32[2]{0:T(128)S(1)} %pad_add_fusion.number_ref, bf16[64,7296]{1,0:T(8,128)(2,1)} %collective-permute-done.25.xa, bf16[64,7296]{1,0:T(8,128)(2,1)} %collective-permute-done.26.xb, bf16[1,7168,256]{2,1,0:T(8,128)(2,1)} %gate_own.7, ...), custom_call_target="tpu_custom_call" | custom-call | tf_op jit(solution)/shard_map/experts/pallas_call | solution.py:240
  154.6 10.2 %experts.4 = (bf16[64,7168]{1,0:T(8,128)(2,1)S(1)}, bf16[64,7168]{1,0:T(8,128)(2,1)S(1)}) custom-call(s32[2]{0:T(128)S(1)} %pad_add_fusion.number_ref, bf16[64,7296]{1,0:T(8,128)(2,1)S(1)} %pad_maximum_fusion.xa, bf16[64,7296]{1,0:T(8,128)(2,1)S(1)} %constant_dynamic-update-slice_fusion.xb, bf16[1,7168,256]{2,1,0:T(8,128)(2,1)} %gate_own.7, ...), custom_call_target="tpu_custom_call" | custom-call | tf_op jit(solution)/shard_map/experts/pallas_call | solution.py:240
  164.8 10.0 %experts.5 = (bf16[64,7168]{1,0:T(8,128)(2,1)S(1)}, bf16[64,7168]{1,0:T(8,128)(2,1)S(1)}) custom-call(s32[2]{0:T(128)S(1)} %pad_add_fusion.number_ref, bf16[64,7296]{1,0:T(8,128)(2,1)} %collective-permute-done.20.xa, bf16[64,7296]{1,0:T(8,128)(2,1)S(1)} %collective-permute-done.21.xb, bf16[1,7168,256]{2,1,0:T(8,128)(2,1)} %gate_own.7, ...), custom_call_target="tpu_custom_call" | custom-call | tf_op jit(solution)/shard_map/experts/pallas_call | solution.py:240
  174.9 3.3 %collective-permute-start.22 = (bf16[64,7168]{1,0:T(8,128)(2,1)S(1)}, bf16[64,7168]{1,0:T(8,128)(2,1)S(1)}, u32[]{:S(2)}, u32[]{:S(2)}) collective-permute-start(bf16[64,7168]{1,0:T(8,128)(2,1)S(1)} %get-tuple-element.22), channel_id=1, source_target_pairs={{0,24},{1,9},{2,26},{3,11},{4,28},{5,13},{6,30},{7,15},{8,0},{9,17... | collective-permute-start | bytes 2752520 | tf_op jit(solution)/shard_map/ppermute | solution.py:55
  178.2 3.7 %collective-permute-start.32 = (bf16[64,7168]{1,0:T(8,128)(2,1)S(1)}, bf16[64,7168]{1,0:T(8,128)(2,1)S(1)}, u32[]{:S(2)}, u32[]{:S(2)}) collective-permute-start(bf16[64,7168]{1,0:T(8,128)(2,1)S(1)} %get-tuple-element.26), channel_id=1, source_target_pairs={{0,6},{1,3},{2,0},{3,5},{4,2},{5,7},{6,4},{7,1},{8,14},{9,11},{10,... | collective-permute-start | bytes 2752520 | tf_op jit(solution)/shard_map/ppermute | solution.py:55
  181.9 10.2 %experts.6 = (bf16[64,7168]{1,0:T(8,128)(2,1)S(1)}, bf16[64,7168]{1,0:T(8,128)(2,1)S(1)}) custom-call(s32[2]{0:T(128)S(1)} %pad_add_fusion.number_ref, bf16[64,7296]{1,0:T(8,128)(2,1)S(1)} %collective-permute-done.23.xa, bf16[64,7296]{1,0:T(8,128)(2,1)S(1)} %collective-permute-done.24.xb, bf16[1,7168,256]{2,1,0:T(8,128)(2,1)} %gate_own.7, ...), custom_call_target="tpu_custom_call" | custom-call | tf_op jit(solution)/shard_map/experts/pallas_call | solution.py:240
  192.5 15.1 %collective-permute-done.33 = bf16[64,7168]{1,0:T(8,128)(2,1)S(1)} collective-permute-done((bf16[64,7168]{1,0:T(8,128)(2,1)S(1)}, bf16[64,7168]{1,0:T(8,128)(2,1)S(1)}, u32[]{:S(2)}, u32[]{:S(2)}) %collective-permute-start.33) | collective-permute-done | bytes 917536 | tf_op jit(solution)/shard_map/ppermute | solution.py:55
  211.6 13.3 %collective-permute-done.34 = bf16[64,7168]{1,0:T(8,128)(2,1)S(1)} collective-permute-done((bf16[64,7168]{1,0:T(8,128)(2,1)S(1)}, bf16[64,7168]{1,0:T(8,128)(2,1)S(1)}, u32[]{:S(2)}, u32[]{:S(2)}) %collective-permute-start.34) | collective-permute-done | bytes 917536 | tf_op jit(solution)/shard_map/ppermute | solution.py:55
  225.4 4.4 %collective-permute-done.29 = bf16[32,7168]{1,0:T(8,128)(2,1)S(1)} collective-permute-done((bf16[32,7168]{1,0:T(8,128)(2,1)S(1)}, bf16[32,7168]{1,0:T(8,128)(2,1)S(1)}, u32[]{:S(2)}, u32[]{:S(2)}) %collective-permute-start.29) | collective-permute-done | bytes 458784 | tf_op jit(solution)/shard_map/ppermute | solution.py:51
  230.0 5.0 %collective-permute-done.35 = bf16[32,7168]{1,0:T(8,128)(2,1)S(1)} collective-permute-done((bf16[32,7168]{1,0:T(8,128)(2,1)S(1)}, bf16[32,7168]{1,0:T(8,128)(2,1)S(1)}, u32[]{:S(2)}, u32[]{:S(2)}) %collective-permute-start.35) | collective-permute-done | bytes 458784 | tf_op jit(solution)/shard_map/ppermute | solution.py:51
  236.4 4.9 %collective-permute-done.36 = bf16[16,7168]{1,0:T(8,128)(2,1)S(1)} collective-permute-done((bf16[16,7168]{1,0:T(8,128)(2,1)S(1)}, bf16[16,7168]{1,0:T(8,128)(2,1)S(1)}, u32[]{:S(2)}, u32[]{:S(2)}) %collective-permute-start.36) | collective-permute-done | bytes 229408 | tf_op jit(solution)/shard_map/ppermute | solution.py:51
  242.6 5.1 %collective-permute-done.37 = bf16[8,7168]{1,0:T(8,128)(2,1)S(1)} collective-permute-done((bf16[8,7168]{1,0:T(8,128)(2,1)S(1)}, bf16[8,7168]{1,0:T(8,128)(2,1)S(1)}, u32[]{:S(2)}, u32[]{:S(2)}) %collective-permute-start.37) | collective-permute-done | bytes 114720 | tf_op jit(solution)/shard_map/ppermute | solution.py:55
  (118 shorter events, 34.3 us)
Async XLA Ops:
  0.0 37.1 %collective-permute-start.1 = (bf16[4,128,7168]{2,1,0:T(8,128)(2,1)}, bf16[4,128,7168]{2,1,0:T(8,128)(2,1)}, u32[]{:S(2)}, u32[]{:S(2)}) collective-permute-start(bf16[4,128,7168]{2,1,0:T(8,128)(2,1)} %param.16), channel_id=1, source_target_pairs={{0,1},{1,0},{2,3},{3,2},{4,5},{5,4},{6,7},{7,6},{8,9},{9,8},{10,11... | collective-permute-start | bytes 22020104 | tf_op jit(solution)/shard_map/ppermute | solution.py:59
  8.0 25.9 %all-to-all-start = ((bf16[16,8,8,512]{3,2,1,0:T(8,128)(2,1)}), bf16[16,8,8,512]{3,2,1,0:T(8,128)(2,1)S(1)}, u32[]{:S(2)}, u32[]{:S(2)}) async-start(bf16[16,8,8,512]{3,2,1,0:T(8,128)(2,1)} %attend.1), calls=%async_computation | async-start | bytes 2097152 | tf_op jit(solution)/shard_map/all_to_all | solution.py:326
  15.5 19.3 %collective-permute-start = (bf16[4,512,128]{1,2,0:T(8,128)(2,1)S(1)}, bf16[4,512,128]{1,2,0:T(8,128)(2,1)S(1)}, u32[]{:S(2)}, u32[]{:S(2)}) collective-permute-start(bf16[4,512,128]{1,2,0:T(8,128)(2,1)S(1)} %copy.15), channel_id=1, source_target_pairs={{0,1},{1,0},{2,3},{3,2},{4,5},{5,4},{6,7},{7,6},{8,9},{9,8},{10,11... | collective-permute-start | bytes 1572872 | tf_op jit(solution)/shard_map/ppermute | solution.py:59
  45.1 10.0 %collective-permute-start.2 = (bf16[64,3584]{1,0:T(8,128)(2,1)}, bf16[64,3584]{1,0:T(8,128)(2,1)S(1)}, u32[]{:S(2)}, u32[]{:S(2)}) collective-permute-start(bf16[64,3584]{1,0:T(8,128)(2,1)} %get-tuple-element.18), channel_id=1, source_target_pairs={{0,24},{1,9},{2,26},{3,11},{4,28},{5,13},{6,30},{7,15},{8,16},{9,1... | collective-permute-start | bytes 1376264 | tf_op jit(solution)/shard_map/ppermute | solution.py:51
  46.0 10.4 %collective-permute-start.6 = (bf16[64,3584]{1,0:T(8,128)(2,1)}, bf16[64,3584]{1,0:T(8,128)(2,1)S(1)}, u32[]{:S(2)}, u32[]{:S(2)}) collective-permute-start(bf16[64,3584]{1,0:T(8,128)(2,1)} %get-tuple-element.20), channel_id=1, source_target_pairs={{0,6},{1,3},{2,4},{3,1},{4,2},{5,7},{6,0},{7,5},{8,14},{9,11},{10,... | collective-permute-start | bytes 1376264 | tf_op jit(solution)/shard_map/ppermute | solution.py:51
  56.5 6.6 %collective-permute-start.7 = (bf16[32,3584]{1,0:T(8,128)(2,1)S(1)}, bf16[32,3584]{1,0:T(8,128)(2,1)S(1)}, u32[]{:S(2)}, u32[]{:S(2)}) collective-permute-start(bf16[32,3584]{1,0:T(8,128)(2,1)S(1)} %slice.103), channel_id=1, source_target_pairs={{0,2},{1,7},{2,0},{3,5},{4,6},{5,3},{6,4},{7,1},{8,10},{9,15},{10,... | collective-permute-start | bytes 688136 | tf_op jit(solution)/shard_map/ppermute | solution.py:51
  62.5 6.7 %collective-permute-start.4 = (bf16[16,3584]{1,0:T(8,128)(2,1)S(1)}, bf16[16,3584]{1,0:T(8,128)(2,1)S(1)}, u32[]{:S(2)}, u32[]{:S(2)}) collective-permute-start(bf16[16,3584]{1,0:T(8,128)(2,1)S(1)} %slice.99), channel_id=1, source_target_pairs={{0,6},{1,3},{2,4},{3,1},{4,2},{5,7},{6,0},{7,5},{8,14},{9,11},{10,... | collective-permute-start | bytes 344072 | tf_op jit(solution)/shard_map/ppermute | solution.py:51
  63.2 6.7 %collective-permute-start.8 = (bf16[16,3584]{1,0:T(8,128)(2,1)S(1)}, bf16[16,3584]{1,0:T(8,128)(2,1)S(1)}, u32[]{:S(2)}, u32[]{:S(2)}) collective-permute-start(bf16[16,3584]{1,0:T(8,128)(2,1)S(1)} %slice.105), channel_id=1, source_target_pairs={{0,24},{1,9},{2,26},{3,11},{4,28},{5,13},{6,30},{7,15},{8,16},{9,1... | collective-permute-start | bytes 344072 | tf_op jit(solution)/shard_map/ppermute | solution.py:51
  74.6 6.8 %collective-permute-start.13 = (bf16[8,7296]{1,0:T(8,128)(2,1)S(1)}, bf16[8,7296]{1,0:T(8,128)(2,1)S(1)}, u32[]{:S(2)}, u32[]{:S(2)}) collective-permute-start(bf16[8,7296]{1,0:T(8,128)(2,1)S(1)} %pad_maximum_fusion.6), channel_id=1, source_target_pairs={{0,64},{1,65},{2,66},{3,67},{4,68},{5,69},{6,70},{7,71},{8,72},{9,... | collective-permute-start | bytes 350216 | tf_op jit(solution)/shard_map/ppermute | solution.py:55
  79.2 47.1 %collective-permute-start.17 = (bf16[1,7168,256]{2,1,0:T(8,128)(2,1)}, bf16[1,7168,256]{2,1,0:T(8,128)(2,1)}, u32[]{:S(2)}, u32[]{:S(2)}) collective-permute-start(bf16[1,7168,256]{2,1,0:T(8,128)(2,1)} %gate_own.7), channel_id=1, source_target_pairs={{0,1},{1,0},{2,3},{3,2},{4,5},{5,4},{6,7},{7,6},{8,9},{9,8},{10,11... | collective-permute-start | bytes 11010056 | tf_op jit(solution)/shard_map/ppermute | solution.py:59
  79.2 51.6 %collective-permute-start.18 = (bf16[1,7168,256]{2,1,0:T(8,128)(2,1)}, bf16[1,7168,256]{2,1,0:T(8,128)(2,1)}, u32[]{:S(2)}, u32[]{:S(2)}) collective-permute-start(bf16[1,7168,256]{2,1,0:T(8,128)(2,1)} %up_own.7), channel_id=1, source_target_pairs={{0,1},{1,0},{2,3},{3,2},{4,5},{5,4},{6,7},{7,6},{8,9},{9,8},{10,11... | collective-permute-start | bytes 11010056 | tf_op jit(solution)/shard_map/ppermute | solution.py:59
  79.7 54.4 %collective-permute-start.19 = (bf16[1,256,7168]{2,1,0:T(8,128)(2,1)}, bf16[1,256,7168]{2,1,0:T(8,128)(2,1)}, u32[]{:S(2)}, u32[]{:S(2)}) collective-permute-start(bf16[1,256,7168]{2,1,0:T(8,128)(2,1)} %down_own.7), channel_id=1, source_target_pairs={{0,1},{1,0},{2,3},{3,2},{4,5},{5,4},{6,7},{7,6},{8,9},{9,8},{10,11... | collective-permute-start | bytes 11010056 | tf_op jit(solution)/shard_map/ppermute | solution.py:59
  81.3 6.5 %collective-permute-start.10 = (bf16[8,7296]{1,0:T(8,128)(2,1)S(1)}, bf16[8,7296]{1,0:T(8,128)(2,1)S(1)}, u32[]{:S(2)}, u32[]{:S(2)}) collective-permute-start(bf16[8,7296]{1,0:T(8,128)(2,1)S(1)} %pad_maximum_fusion.6), channel_id=1, source_target_pairs={{0,32},{1,97},{2,34},{3,99},{4,36},{5,101},{6,38},{7,103},{8,40},{... | collective-permute-start | bytes 350216 | tf_op jit(solution)/shard_map/ppermute | solution.py:55
  84.3 6.8 %collective-permute-start.15 = (bf16[16,7296]{1,0:T(8,128)(2,1)S(1)}, bf16[16,7296]{1,0:T(8,128)(2,1)S(1)}, u32[]{:S(2)}, u32[]{:S(2)}) collective-permute-start(bf16[16,7296]{1,0:T(8,128)(2,1)S(1)} %pad_maximum_fusion.5), channel_id=1, source_target_pairs={{0,8},{1,25},{2,10},{3,27},{4,12},{5,29},{6,14},{7,31},{8,0},{9,17... | collective-permute-start | bytes 700424 | tf_op jit(solution)/shard_map/ppermute | solution.py:51
  87.9 6.6 %collective-permute-start.11 = (bf16[16,7296]{1,0:T(8,128)(2,1)S(1)}, bf16[16,7296]{1,0:T(8,128)(2,1)S(1)}, u32[]{:S(2)}, u32[]{:S(2)}) collective-permute-start(bf16[16,7296]{1,0:T(8,128)(2,1)S(1)} %pad_maximum_fusion.4), channel_id=1, source_target_pairs={{0,2},{1,7},{2,0},{3,5},{4,6},{5,3},{6,4},{7,1},{8,10},{9,15},{10,... | collective-permute-start | bytes 700424 | tf_op jit(solution)/shard_map/ppermute | solution.py:51
  91.2 9.9 %collective-permute-start.16 = (bf16[32,7296]{1,0:T(8,128)(2,1)S(1)}, bf16[32,7296]{1,0:T(8,128)(2,1)S(1)}, u32[]{:S(2)}, u32[]{:S(2)}) collective-permute-start(bf16[32,7296]{1,0:T(8,128)(2,1)S(1)} %pad_maximum_fusion.2), channel_id=1, source_target_pairs={{0,24},{1,9},{2,26},{3,11},{4,28},{5,13},{6,30},{7,15},{8,16},{9,1... | collective-permute-start | bytes 1400840 | tf_op jit(solution)/shard_map/ppermute | solution.py:51
  94.5 13.8 %collective-permute-start.12 = (bf16[32,7296]{1,0:T(8,128)(2,1)S(1)}, bf16[32,7296]{1,0:T(8,128)(2,1)S(1)}, u32[]{:S(2)}, u32[]{:S(2)}) collective-permute-start(bf16[32,7296]{1,0:T(8,128)(2,1)S(1)} %pad_maximum_fusion.1), channel_id=1, source_target_pairs={{0,6},{1,3},{2,4},{3,1},{4,2},{5,7},{6,0},{7,5},{8,14},{9,11},{10,... | collective-permute-start | bytes 1400840 | tf_op jit(solution)/shard_map/ppermute | solution.py:51
  101.1 14.8 %collective-permute-start.21 = (bf16[64,7296]{1,0:T(8,128)(2,1)S(1)}, bf16[64,7296]{1,0:T(8,128)(2,1)S(1)}, u32[]{:S(2)}, u32[]{:S(2)}) collective-permute-start(bf16[64,7296]{1,0:T(8,128)(2,1)S(1)} %constant_dynamic-update-slice_fusion.xb), channel_id=1, source_target_pairs={{0,2},{1,7},{2,4},{3,1},{4,6},{5,3},{6,0},{7,5},{8,10},{9,15},{10,... | collective-permute-start | bytes 2801672 | tf_op jit(solution)/shard_map/ppermute | solution.py:55
  108.4 17.9 %collective-permute-start.20 = (bf16[64,7296]{1,0:T(8,128)(2,1)S(1)}, bf16[64,7296]{1,0:T(8,128)(2,1)}, u32[]{:S(2)}, u32[]{:S(2)}) collective-permute-start(bf16[64,7296]{1,0:T(8,128)(2,1)S(1)} %pad_maximum_fusion.xa), channel_id=1, source_target_pairs={{0,8},{1,25},{2,10},{3,27},{4,12},{5,29},{6,14},{7,31},{8,16},{9,1... | collective-permute-start | bytes 2801672 | tf_op jit(solution)/shard_map/ppermute | solution.py:55
  115.9 24.4 %collective-permute-start.26 = (bf16[64,7296]{1,0:T(8,128)(2,1)S(1)}, bf16[64,7296]{1,0:T(8,128)(2,1)}, u32[]{:S(2)}, u32[]{:S(2)}) collective-permute-start(bf16[64,7296]{1,0:T(8,128)(2,1)S(1)} %collective-permute-done.21.xb), channel_id=1, source_target_pairs={{0,2},{1,7},{2,4},{3,1},{4,6},{5,3},{6,0},{7,5},{8,10},{9,15},{10,... | collective-permute-start | bytes 2801672 | tf_op jit(solution)/shard_map/ppermute | solution.py:55
  126.3 17.1 %collective-permute-start.25 = (bf16[64,7296]{1,0:T(8,128)(2,1)}, bf16[64,7296]{1,0:T(8,128)(2,1)}, u32[]{:S(2)}, u32[]{:S(2)}) collective-permute-start(bf16[64,7296]{1,0:T(8,128)(2,1)} %collective-permute-done.20.xa), channel_id=1, source_target_pairs={{0,8},{1,25},{2,10},{3,27},{4,12},{5,29},{6,14},{7,31},{8,16},{9,1... | collective-permute-start | bytes 2801672 | tf_op jit(solution)/shard_map/ppermute | solution.py:55
  126.3 55.5 %collective-permute-start.24 = (bf16[64,7296]{1,0:T(8,128)(2,1)S(1)}, bf16[64,7296]{1,0:T(8,128)(2,1)S(1)}, u32[]{:S(2)}, u32[]{:S(2)}) collective-permute-start(bf16[64,7296]{1,0:T(8,128)(2,1)S(1)} %constant_dynamic-update-slice_fusion.xb), channel_id=1, source_target_pairs={{0,6},{1,3},{2,0},{3,5},{4,2},{5,7},{6,4},{7,1},{8,14},{9,11},{10,... | collective-permute-start | bytes 2801672 | tf_op jit(solution)/shard_map/ppermute | solution.py:55
  130.8 51.0 %collective-permute-start.23 = (bf16[64,7296]{1,0:T(8,128)(2,1)S(1)}, bf16[64,7296]{1,0:T(8,128)(2,1)S(1)}, u32[]{:S(2)}, u32[]{:S(2)}) collective-permute-start(bf16[64,7296]{1,0:T(8,128)(2,1)S(1)} %pad_maximum_fusion.xa), channel_id=1, source_target_pairs={{0,24},{1,9},{2,26},{3,11},{4,28},{5,13},{6,30},{7,15},{8,0},{9,17... | collective-permute-start | bytes 2801672 | tf_op jit(solution)/shard_map/ppermute | solution.py:55
  154.5 37.6 %collective-permute-start.27 = (bf16[64,7168]{1,0:T(8,128)(2,1)S(1)}, bf16[64,7168]{1,0:T(8,128)(2,1)S(1)}, u32[]{:S(2)}, u32[]{:S(2)}) collective-permute-start(bf16[64,7168]{1,0:T(8,128)(2,1)S(1)} %get-tuple-element.24), channel_id=1, source_target_pairs={{0,8},{1,25},{2,10},{3,27},{4,12},{5,29},{6,14},{7,31},{8,16},{9,1... | collective-permute-start | bytes 2752520 | tf_op jit(solution)/shard_map/ppermute | solution.py:55
  174.9 35.4 %collective-permute-start.22 = (bf16[64,7168]{1,0:T(8,128)(2,1)S(1)}, bf16[64,7168]{1,0:T(8,128)(2,1)S(1)}, u32[]{:S(2)}, u32[]{:S(2)}) collective-permute-start(bf16[64,7168]{1,0:T(8,128)(2,1)S(1)} %get-tuple-element.22), channel_id=1, source_target_pairs={{0,24},{1,9},{2,26},{3,11},{4,28},{5,13},{6,30},{7,15},{8,0},{9,17... | collective-permute-start | bytes 2752520 | tf_op jit(solution)/shard_map/ppermute | solution.py:55
  178.2 33.4 %collective-permute-start.32 = (bf16[64,7168]{1,0:T(8,128)(2,1)S(1)}, bf16[64,7168]{1,0:T(8,128)(2,1)S(1)}, u32[]{:S(2)}, u32[]{:S(2)}) collective-permute-start(bf16[64,7168]{1,0:T(8,128)(2,1)S(1)} %get-tuple-element.26), channel_id=1, source_target_pairs={{0,6},{1,3},{2,0},{3,5},{4,2},{5,7},{6,4},{7,1},{8,14},{9,11},{10,... | collective-permute-start | bytes 2752520 | tf_op jit(solution)/shard_map/ppermute | solution.py:55
  192.1 15.5 %collective-permute-start.33 = (bf16[64,7168]{1,0:T(8,128)(2,1)S(1)}, bf16[64,7168]{1,0:T(8,128)(2,1)S(1)}, u32[]{:S(2)}, u32[]{:S(2)}) collective-permute-start(bf16[64,7168]{1,0:T(8,128)(2,1)S(1)} %get-tuple-element.28), channel_id=1, source_target_pairs={{0,2},{1,7},{2,4},{3,1},{4,6},{5,3},{6,0},{7,5},{8,10},{9,15},{10,... | collective-permute-start | bytes 2752520 | tf_op jit(solution)/shard_map/ppermute | solution.py:55
  192.4 17.9 %collective-permute-start.28 = (bf16[64,7168]{1,0:T(8,128)(2,1)S(1)}, bf16[64,7168]{1,0:T(8,128)(2,1)S(1)}, u32[]{:S(2)}, u32[]{:S(2)}) collective-permute-start(bf16[64,7168]{1,0:T(8,128)(2,1)S(1)} %add_convert_fusion.3), channel_id=1, source_target_pairs={{0,8},{1,25},{2,10},{3,27},{4,12},{5,29},{6,14},{7,31},{8,16},{9,1... | collective-permute-start | bytes 2752520 | tf_op jit(solution)/shard_map/ppermute | solution.py:55
  207.8 17.1 %collective-permute-start.34 = (bf16[64,7168]{1,0:T(8,128)(2,1)S(1)}, bf16[64,7168]{1,0:T(8,128)(2,1)S(1)}, u32[]{:S(2)}, u32[]{:S(2)}) collective-permute-start(bf16[64,7168]{1,0:T(8,128)(2,1)S(1)} %add_convert_fusion.1), channel_id=1, source_target_pairs={{0,2},{1,7},{2,4},{3,1},{4,6},{5,3},{6,0},{7,5},{8,10},{9,15},{10,... | collective-permute-start | bytes 2752520 | tf_op jit(solution)/shard_map/ppermute | solution.py:55
  210.7 19.1 %collective-permute-start.29 = (bf16[32,7168]{1,0:T(8,128)(2,1)S(1)}, bf16[32,7168]{1,0:T(8,128)(2,1)S(1)}, u32[]{:S(2)}, u32[]{:S(2)}) collective-permute-start(bf16[32,7168]{1,0:T(8,128)(2,1)S(1)} %slice.109), channel_id=1, source_target_pairs={{0,6},{1,3},{2,4},{3,1},{4,2},{5,7},{6,0},{7,5},{8,14},{9,11},{10,... | collective-permute-start | bytes 1376264 | tf_op jit(solution)/shard_map/ppermute | solution.py:51
  225.3 9.8 %collective-permute-start.35 = (bf16[32,7168]{1,0:T(8,128)(2,1)S(1)}, bf16[32,7168]{1,0:T(8,128)(2,1)S(1)}, u32[]{:S(2)}, u32[]{:S(2)}) collective-permute-start(bf16[32,7168]{1,0:T(8,128)(2,1)S(1)} %slice.115), channel_id=1, source_target_pairs={{0,24},{1,9},{2,26},{3,11},{4,28},{5,13},{6,30},{7,15},{8,16},{9,1... | collective-permute-start | bytes 1376264 | tf_op jit(solution)/shard_map/ppermute | solution.py:51
  236.1 6.5 %collective-permute-start.31 = (bf16[8,7168]{1,0:T(8,128)(2,1)S(1)}, bf16[8,7168]{1,0:T(8,128)(2,1)S(1)}, u32[]{:S(2)}, u32[]{:S(2)}) collective-permute-start(bf16[8,7168]{1,0:T(8,128)(2,1)S(1)} %slice.113), channel_id=1, source_target_pairs={{0,96},{1,33},{2,98},{3,35},{4,100},{5,37},{6,102},{7,39},{8,104},... | collective-permute-start | bytes 344072 | tf_op jit(solution)/shard_map/ppermute | solution.py:55
  (13 other events, 99.1 us)
where the time goes:
time: 250 us
  waiting for transfers between devices  136 us (54%)
  Pallas kernels  57.6 us (23%)
  starting transfers between devices  48 us (19%)
  other arithmetic  4.29 us (2%)
  matrix products  2.6 us (1%)
    ppermute x18, waiting for transfers between devices, onward(): return lax.ppermute(value, ALL, ring_next(axis, hops))  68 us
    ppermute x16, waiting for transfers between devices, swap(): return lax.ppermute(value, ALL, ring_pairs(axis, step))  49.6 us
    pallas_call x4, Pallas kernels, experts(): pl.pallas_call(experts_kernel, in_specs=[pl.BlockSpec(memory_space=pltpu....  41.6 us
    ppermute x18, starting transfers between devices, onward(): return lax.ppermute(value, ALL, ring_next(axis, hops))  27.2 us
    all_to_all x1, waiting for transfers between devices, run_rows(): lax.all_to_all(heads_out, 'dev', split_axis=0, concat_axis=0, tiled=True,...  18.1 us
    ppermute x16, starting transfers between devices, swap(): return lax.ppermute(value, ALL, ring_pairs(axis, step))  12.7 us
    pallas_call x1, Pallas kernels, project(): pl.pallas_call(lambda *refs: project_kernel(steps, *refs), grid=(2 * step...  8.02 us
    pallas_call x1, Pallas kernels, attend(): pl.pallas_call(lambda *refs: attend_kernel(first, *refs), grid_spec=pltpu...  8 us
  transfers between devices with their start and end apart: 40, of which 27 were waited for; matrix products, arithmetic and copies ran while one was open for 3% of the time, Pallas kernels for 20%

commit v1 on v0

--- a/solution.py
+++ b/solution.py
@@ -375,29 +375,20 @@
 
     numbers = jnp.stack([device, device ^ 1]).astype(jnp.int32)
     weights = (w_gate, w_up, gate_other, up_other, w_down, down_other)
-
-    def both(pair, hops):
-        moved_on = []
-        for at, axis in enumerate((Y, X)):
-            moved_on.append(onward(pair[at], axis, hops))
-        return moved_on
-
     held = [(first, second)]
-    held.append(both(held[0], 1))
-    from_ahead = both(held[0], 3)
-    held.append(both(held[1], 1))
-    held.append(from_ahead)
+    for _ in range(1, 4):
+        one = onward(held[-1][0], Y)
+        two = onward(held[-1][1], X)
+        held.append((one, two))
     done = []
     for hop in range(4):
         done.append(experts(numbers, *held[hop], weights, width))
-    near = both(done[1], 3)
-    far = both(done[2], 1)
-    far = [add(done[3][at], far[at]) for at in range(2)]
-    far = both(far, 1)
-    one, two = [
-        (done[0][at].astype(F32) + near[at].astype(F32) + far[at].astype(F32)).astype(BF)
-        for at in range(2)
-    ]
+    one, two = done[1]
+    for hop in range(1, 4):
+        one = onward(one, Y)
+        two = onward(two, X)
+        one = add(one, done[(hop + 1) % 4][0])
+        two = add(two, done[(hop + 1) % 4][1])
     for step in (1, 0):
         one = fold(one, X, step)
         two = fold(two, Y, step)

time: 250 us -> 236 us (0.944)
  the two profiles are of different devices: /device:TPU:0 before, /device:TPU:24 now
where the time goes in v1:
time: 236 us
  waiting for transfers between devices  132 us (56%)
  Pallas kernels  56.7 us (24%)
  starting transfers between devices  38.4 us (16%)
  other arithmetic  4.51 us (2%)
  matrix products  2.6 us (1%)
    ppermute x18, waiting for transfers between devices, onward(): return lax.ppermute(value, ALL, ring_next(axis, hops))  60.5 us
    ppermute x16, waiting for transfers between devices, swap(): return lax.ppermute(value, ALL, ring_pairs(axis, step))  55.5 us
    pallas_call x4, Pallas kernels, experts(): pl.pallas_call(experts_kernel, in_specs=[pl.BlockSpec(memory_space=pltpu....  40.7 us
    ppermute x18, starting transfers between devices, onward(): return lax.ppermute(value, ALL, ring_next(axis, hops))  21.9 us
    all_to_all x1, waiting for transfers between devices, run_rows(): lax.all_to_all(heads_out, 'dev', split_axis=0, concat_axis=0, tiled=True,...  15.7 us
    ppermute x16, starting transfers between devices, swap(): return lax.ppermute(value, ALL, ring_pairs(axis, step))  8.63 us
    pallas_call x1, Pallas kernels, project(): pl.pallas_call(lambda *refs: project_kernel(steps, *refs), grid=(2 * step...  8.02 us
    pallas_call x1, Pallas kernels, attend(): pl.pallas_call(lambda *refs: attend_kernel(first, *refs), grid_spec=pltpu...  8 us
  transfers between devices with their start and end apart: 40, of which 29 were waited for; matrix products, arithmetic and copies ran while one was open for 3% of the time, Pallas kernels for 21%

profile of v1, /device:TPU:24, one launch (start us, length us, event | category | flops | bytes accessed | tf_op | source)
XLA Modules:
  0.0 235.5 jit_solution(4868825960804259054)
XLA Ops:
  0.0 8.0 %attend.1 = bf16[16,8,8,512]{3,2,1,0:T(8,128)(2,1)} custom-call(s32[8]{0:T(128)} %refs_0_.1, bf16[8,576,128]{2,1,0:T(8,128)(2,1)} %bitcast.21, bf16[8,576,512]{2,1,0:T(8,128)(2,1)} %bitcast.17), custom_call_target="tpu_custom_call" | custom-call | tf_op jit(solution)/shard_map/attend/pallas_call | solution.py:88
  8.0 7.3 %all-to-all-start = ((bf16[16,8,8,512]{3,2,1,0:T(8,128)(2,1)}), bf16[16,8,8,512]{3,2,1,0:T(8,128)(2,1)S(1)}, u32[]{:S(2)}, u32[]{:S(2)}) async-start(bf16[16,8,8,512]{3,2,1,0:T(8,128)(2,1)} %attend.1), calls=%async_computation | async-start | bytes 2097152 | tf_op jit(solution)/shard_map/all_to_all | solution.py:326
  15.7 15.7 %all-to-all-done = bf16[16,8,8,512]{3,2,1,0:T(8,128)(2,1)S(1)} async-done(((bf16[16,8,8,512]{3,2,1,0:T(8,128)(2,1)}), bf16[16,8,8,512]{3,2,1,0:T(8,128)(2,1)S(1)}, u32[]{:S(2)}, u32[]{:S(2)}) %all-to-all-start) | async-done | bytes 1048608 | tf_op jit(solution)/shard_map/all_to_all | solution.py:326
  34.6 8.0 %project.1 = (bf16[64,3584]{1,0:T(8,128)(2,1)}, bf16[64,3584]{1,0:T(8,128)(2,1)}, bf16[64,3584]{1,0:T(8,128)(2,1)}, bf16[64,3584]{1,0:T(8,128)(2,1)}) custom-call(bf16[128,1024]{1,0:T(8,128)(2,1)} %convolution_convert_fusion.1.refs_0_, bf16[128,1024]{1,0:T(8,128)(2,1)} %convolution_convert_fusion.refs_1_, bf16[512,7168]{1,0:T(8,128)(2,1)} %bitcast.16, ...), custom_call_target="tpu_custom_call" | custom-call | tf_op jit(solution)/shard_map/project/pallas_call | solution.py:133
  42.7 2.7 %collective-permute-start.2 = (bf16[64,3584]{1,0:T(8,128)(2,1)}, bf16[64,3584]{1,0:T(8,128)(2,1)S(1)}, u32[]{:S(2)}, u32[]{:S(2)}) collective-permute-start(bf16[64,3584]{1,0:T(8,128)(2,1)} %get-tuple-element.18), channel_id=1, source_target_pairs={{0,24},{1,9},{2,26},{3,11},{4,28},{5,13},{6,30},{7,15},{8,16},{9,1... | collective-permute-start | bytes 1376264 | tf_op jit(solution)/shard_map/ppermute | solution.py:51
  45.5 7.2 %collective-permute-done.2 = bf16[64,3584]{1,0:T(8,128)(2,1)S(1)} collective-permute-done((bf16[64,3584]{1,0:T(8,128)(2,1)}, bf16[64,3584]{1,0:T(8,128)(2,1)S(1)}, u32[]{:S(2)}, u32[]{:S(2)}) %collective-permute-start.2) | collective-permute-done | bytes 458784 | tf_op jit(solution)/shard_map/ppermute | solution.py:51
  55.6 4.3 %collective-permute-done.3 = bf16[32,3584]{1,0:T(8,128)(2,1)S(1)} collective-permute-done((bf16[32,3584]{1,0:T(8,128)(2,1)S(1)}, bf16[32,3584]{1,0:T(8,128)(2,1)S(1)}, u32[]{:S(2)}, u32[]{:S(2)}) %collective-permute-start.3) | collective-permute-done | bytes 229408 | tf_op jit(solution)/shard_map/ppermute | solution.py:51
  63.4 2.6 %collective-permute-done.4 = bf16[16,3584]{1,0:T(8,128)(2,1)S(1)} collective-permute-done((bf16[16,3584]{1,0:T(8,128)(2,1)S(1)}, bf16[16,3584]{1,0:T(8,128)(2,1)S(1)}, u32[]{:S(2)}, u32[]{:S(2)}) %collective-permute-start.4) | collective-permute-done | bytes 114720 | tf_op jit(solution)/shard_map/ppermute | solution.py:51
  66.2 2.8 %collective-permute-done.8 = bf16[16,3584]{1,0:T(8,128)(2,1)S(1)} collective-permute-done((bf16[16,3584]{1,0:T(8,128)(2,1)S(1)}, bf16[16,3584]{1,0:T(8,128)(2,1)S(1)}, u32[]{:S(2)}, u32[]{:S(2)}) %collective-permute-start.8) | collective-permute-done | bytes 114720 | tf_op jit(solution)/shard_map/ppermute | solution.py:51
  70.4 3.0 %collective-permute-done.9 = bf16[8,3584]{1,0:T(8,128)(2,1)S(1)} collective-permute-done((bf16[8,3584]{1,0:T(8,128)(2,1)S(1)}, bf16[8,3584]{1,0:T(8,128)(2,1)S(1)}, u32[]{:S(2)}, u32[]{:S(2)}) %collective-permute-start.9) | collective-permute-done | bytes 57376 | tf_op jit(solution)/shard_map/ppermute | solution.py:51
  73.7 3.9 %collective-permute-start.14 = (bf16[8,7296]{1,0:T(8,128)(2,1)S(1)}, bf16[8,7296]{1,0:T(8,128)(2,1)S(1)}, u32[]{:S(2)}, u32[]{:S(2)}) collective-permute-start(bf16[8,7296]{1,0:T(8,128)(2,1)S(1)} %pad_maximum_fusion.6), channel_id=1, source_target_pairs={{0,64},{1,65},{2,66},{3,67},{4,68},{5,69},{6,70},{7,71},{8,72},{9,... | collective-permute-start | bytes 350216 | tf_op jit(solution)/shard_map/ppermute | solution.py:55
  80.3 1.7 collective-permute-start.10
  83.4 3.6 %collective-permute-done.10 = bf16[8,7296]{1,0:T(8,128)(2,1)S(1)} collective-permute-done((bf16[8,7296]{1,0:T(8,128)(2,1)S(1)}, bf16[8,7296]{1,0:T(8,128)(2,1)S(1)}, u32[]{:S(2)}, u32[]{:S(2)}) %collective-permute-start.10) | collective-permute-done | bytes 116768 | tf_op jit(solution)/shard_map/ppermute | solution.py:55
  87.1 3.1 %collective-permute-done.16 = bf16[16,7296]{1,0:T(8,128)(2,1)S(1)} collective-permute-done((bf16[16,7296]{1,0:T(8,128)(2,1)S(1)}, bf16[16,7296]{1,0:T(8,128)(2,1)S(1)}, u32[]{:S(2)}, u32[]{:S(2)}) %collective-permute-start.16) | collective-permute-done | bytes 233504 | tf_op jit(solution)/shard_map/ppermute | solution.py:51
  91.4 2.2 collective-permute-done.11
  94.3 5.8 %collective-permute-done.17 = bf16[32,7296]{1,0:T(8,128)(2,1)S(1)} collective-permute-done((bf16[32,7296]{1,0:T(8,128)(2,1)S(1)}, bf16[32,7296]{1,0:T(8,128)(2,1)S(1)}, u32[]{:S(2)}, u32[]{:S(2)}) %collective-permute-start.17) | collective-permute-done | bytes 466976 | tf_op jit(solution)/shard_map/ppermute | solution.py:51
  100.4 5.0 %collective-permute-done.12 = bf16[32,7296]{1,0:T(8,128)(2,1)S(1)} collective-permute-done((bf16[32,7296]{1,0:T(8,128)(2,1)S(1)}, bf16[32,7296]{1,0:T(8,128)(2,1)S(1)}, u32[]{:S(2)}, u32[]{:S(2)}) %collective-permute-start.12) | collective-permute-done | bytes 466976 | tf_op jit(solution)/shard_map/ppermute | solution.py:51
  105.5 3.1 %collective-permute-start.13 = (bf16[64,7296]{1,0:T(8,128)(2,1)S(1)}, bf16[64,7296]{1,0:T(8,128)(2,1)}, u32[]{:S(2)}, u32[]{:S(2)}) collective-permute-start(bf16[64,7296]{1,0:T(8,128)(2,1)S(1)} %pad_maximum_fusion.xa), channel_id=1, source_target_pairs={{0,8},{1,25},{2,10},{3,27},{4,12},{5,29},{6,14},{7,31},{8,16},{9,1... | collective-permute-start | bytes 2801672 | tf_op jit(solution)/shard_map/ppermute | solution.py:55
  108.6 6.4 %collective-permute-done.18.xb = bf16[64,7296]{1,0:T(8,128)(2,1)S(1)} collective-permute-done((bf16[64,7296]{1,0:T(8,128)(2,1)S(1)}, bf16[64,7296]{1,0:T(8,128)(2,1)S(1)}, u32[]{:S(2)}, u32[]{:S(2)}) %collective-permute-start.18) | collective-permute-done | bytes 933920 | tf_op jit(solution)/shard_map/ppermute | solution.py:55
  115.0 4.7 %collective-permute-done.13.xa = bf16[64,7296]{1,0:T(8,128)(2,1)} collective-permute-done((bf16[64,7296]{1,0:T(8,128)(2,1)S(1)}, bf16[64,7296]{1,0:T(8,128)(2,1)}, u32[]{:S(2)}, u32[]{:S(2)}) %collective-permute-start.13) | collective-permute-done | bytes 933920 | tf_op jit(solution)/shard_map/ppermute | solution.py:55
  119.7 3.8 %collective-permute-start.23 = (bf16[64,7296]{1,0:T(8,128)(2,1)}, bf16[64,7296]{1,0:T(8,128)(2,1)S(1)}, u32[]{:S(2)}, u32[]{:S(2)}) collective-permute-start(bf16[64,7296]{1,0:T(8,128)(2,1)} %collective-permute-done.13.xa), channel_id=1, source_target_pairs={{0,8},{1,25},{2,10},{3,27},{4,12},{5,29},{6,14},{7,31},{8,16},{9,1... | collective-permute-start | bytes 2801672 | tf_op jit(solution)/shard_map/ppermute | solution.py:55
  123.6 10.0 %experts.4 = (bf16[64,7168]{1,0:T(8,128)(2,1)S(1)}, bf16[64,7168]{1,0:T(8,128)(2,1)S(1)}) custom-call(s32[2]{0:T(128)S(1)} %pad_add_fusion.number_ref, bf16[64,7296]{1,0:T(8,128)(2,1)} %collective-permute-done.13.xa, bf16[64,7296]{1,0:T(8,128)(2,1)S(1)} %collective-permute-done.18.xb, bf16[1,7168,256]{2,1,0:T(8,128)(2,1)} %gate_own.7, ...), custom_call_target="tpu_custom_call" | custom-call | tf_op jit(solution)/shard_map/experts/pallas_call | solution.py:240
  133.7 10.2 %experts.7 = (bf16[64,7168]{1,0:T(8,128)(2,1)S(1)}, bf16[64,7168]{1,0:T(8,128)(2,1)S(1)}) custom-call(s32[2]{0:T(128)S(1)} %pad_add_fusion.number_ref, bf16[64,7296]{1,0:T(8,128)(2,1)S(1)} %pad_maximum_fusion.xa, bf16[64,7296]{1,0:T(8,128)(2,1)S(1)} %constant_dynamic-update-slice_fusion.xb, bf16[1,7168,256]{2,1,0:T(8,128)(2,1)} %gate_own.7, ...), custom_call_target="tpu_custom_call" | custom-call | tf_op jit(solution)/shard_map/experts/pallas_call | solution.py:240
  143.9 2.2 collective-permute-start.32
  146.2 10.2 %experts.5 = (bf16[64,7168]{1,0:T(8,128)(2,1)S(1)}, bf16[64,7168]{1,0:T(8,128)(2,1)S(1)}) custom-call(s32[2]{0:T(128)S(1)} %pad_add_fusion.number_ref, bf16[64,7296]{1,0:T(8,128)(2,1)S(1)} %collective-permute-done.23.xa, bf16[64,7296]{1,0:T(8,128)(2,1)S(1)} %collective-permute-done.24.xb, bf16[1,7168,256]{2,1,0:T(8,128)(2,1)} %gate_own.7, ...), custom_call_target="tpu_custom_call" | custom-call | tf_op jit(solution)/shard_map/experts/pallas_call | solution.py:240
  160.8 10.8 %collective-permute-done.27.xb = bf16[64,7296]{1,0:T(8,128)(2,1)S(1)} collective-permute-done((bf16[64,7296]{1,0:T(8,128)(2,1)S(1)}, bf16[64,7296]{1,0:T(8,128)(2,1)S(1)}, u32[]{:S(2)}, u32[]{:S(2)}) %collective-permute-start.27) | collective-permute-done | bytes 933920 | tf_op jit(solution)/shard_map/ppermute | solution.py:55
  171.5 8.5 %collective-permute-done.26.xa = bf16[64,7296]{1,0:T(8,128)(2,1)S(1)} collective-permute-done((bf16[64,7296]{1,0:T(8,128)(2,1)S(1)}, bf16[64,7296]{1,0:T(8,128)(2,1)S(1)}, u32[]{:S(2)}, u32[]{:S(2)}) %collective-permute-start.26) | collective-permute-done | bytes 933920 | tf_op jit(solution)/shard_map/ppermute | solution.py:55
  180.1 10.2 %experts.6 = (bf16[64,7168]{1,0:T(8,128)(2,1)S(1)}, bf16[64,7168]{1,0:T(8,128)(2,1)S(1)}) custom-call(s32[2]{0:T(128)S(1)} %pad_add_fusion.number_ref, bf16[64,7296]{1,0:T(8,128)(2,1)S(1)} %collective-permute-done.26.xa, bf16[64,7296]{1,0:T(8,128)(2,1)S(1)} %collective-permute-done.27.xb, bf16[1,7168,256]{2,1,0:T(8,128)(2,1)} %gate_own.7, ...), custom_call_target="tpu_custom_call" | custom-call | tf_op jit(solution)/shard_map/experts/pallas_call | solution.py:240
  192.1 16.8 %collective-permute-done.28 = bf16[64,7168]{1,0:T(8,128)(2,1)S(1)} collective-permute-done((bf16[64,7168]{1,0:T(8,128)(2,1)S(1)}, bf16[64,7168]{1,0:T(8,128)(2,1)S(1)}, u32[]{:S(2)}, u32[]{:S(2)}) %collective-permute-start.28) | collective-permute-done | bytes 917536 | tf_op jit(solution)/shard_map/ppermute | solution.py:55
  211.2 7.8 %collective-permute-done.29 = bf16[32,7168]{1,0:T(8,128)(2,1)S(1)} collective-permute-done((bf16[32,7168]{1,0:T(8,128)(2,1)S(1)}, bf16[32,7168]{1,0:T(8,128)(2,1)S(1)}, u32[]{:S(2)}, u32[]{:S(2)}) %collective-permute-start.29) | collective-permute-done | bytes 458784 | tf_op jit(solution)/shard_map/ppermute | solution.py:51
  221.1 4.1 %collective-permute-done.30 = bf16[16,7168]{1,0:T(8,128)(2,1)S(1)} collective-permute-done((bf16[16,7168]{1,0:T(8,128)(2,1)S(1)}, bf16[16,7168]{1,0:T(8,128)(2,1)S(1)}, u32[]{:S(2)}, u32[]{:S(2)}) %collective-permute-start.30) | collective-permute-done | bytes 229408 | tf_op jit(solution)/shard_map/ppermute | solution.py:51
  230.1 3.4 %collective-permute-done.37 = bf16[8,7168]{1,0:T(8,128)(2,1)S(1)} collective-permute-done((bf16[8,7168]{1,0:T(8,128)(2,1)S(1)}, bf16[8,7168]{1,0:T(8,128)(2,1)S(1)}, u32[]{:S(2)}, u32[]{:S(2)}) %collective-permute-start.37) | collective-permute-done | bytes 114720 | tf_op jit(solution)/shard_map/ppermute | solution.py:55
  (120 shorter events, 35.9 us)
Async XLA Ops:
  0.0 34.6 %collective-permute-start.1 = (bf16[4,128,7168]{2,1,0:T(8,128)(2,1)}, bf16[4,128,7168]{2,1,0:T(8,128)(2,1)}, u32[]{:S(2)}, u32[]{:S(2)}) collective-permute-start(bf16[4,128,7168]{2,1,0:T(8,128)(2,1)} %param.16), channel_id=1, source_target_pairs={{0,1},{1,0},{2,3},{3,2},{4,5},{5,4},{6,7},{7,6},{8,9},{9,8},{10,11... | collective-permute-start | bytes 22020104 | tf_op jit(solution)/shard_map/ppermute | solution.py:59
  8.0 23.4 %all-to-all-start = ((bf16[16,8,8,512]{3,2,1,0:T(8,128)(2,1)}), bf16[16,8,8,512]{3,2,1,0:T(8,128)(2,1)S(1)}, u32[]{:S(2)}, u32[]{:S(2)}) async-start(bf16[16,8,8,512]{3,2,1,0:T(8,128)(2,1)} %attend.1), calls=%async_computation | async-start | bytes 2097152 | tf_op jit(solution)/shard_map/all_to_all | solution.py:326
  15.5 16.8 %collective-permute-start = (bf16[4,512,128]{1,2,0:T(8,128)(2,1)S(1)}, bf16[4,512,128]{1,2,0:T(8,128)(2,1)S(1)}, u32[]{:S(2)}, u32[]{:S(2)}) collective-permute-start(bf16[4,512,128]{1,2,0:T(8,128)(2,1)S(1)} %copy.15), channel_id=1, source_target_pairs={{0,1},{1,0},{2,3},{3,2},{4,5},{5,4},{6,7},{7,6},{8,9},{9,8},{10,11... | collective-permute-start | bytes 1572872 | tf_op jit(solution)/shard_map/ppermute | solution.py:59
  42.7 10.0 %collective-permute-start.2 = (bf16[64,3584]{1,0:T(8,128)(2,1)}, bf16[64,3584]{1,0:T(8,128)(2,1)S(1)}, u32[]{:S(2)}, u32[]{:S(2)}) collective-permute-start(bf16[64,3584]{1,0:T(8,128)(2,1)} %get-tuple-element.18), channel_id=1, source_target_pairs={{0,24},{1,9},{2,26},{3,11},{4,28},{5,13},{6,30},{7,15},{8,16},{9,1... | collective-permute-start | bytes 1376264 | tf_op jit(solution)/shard_map/ppermute | solution.py:51
  45.4 9.9 %collective-permute-start.6 = (bf16[64,3584]{1,0:T(8,128)(2,1)}, bf16[64,3584]{1,0:T(8,128)(2,1)S(1)}, u32[]{:S(2)}, u32[]{:S(2)}) collective-permute-start(bf16[64,3584]{1,0:T(8,128)(2,1)} %get-tuple-element.20), channel_id=1, source_target_pairs={{0,6},{1,3},{2,4},{3,1},{4,2},{5,7},{6,0},{7,5},{8,14},{9,11},{10,... | collective-permute-start | bytes 1376264 | tf_op jit(solution)/shard_map/ppermute | solution.py:51
  53.8 6.1 %collective-permute-start.3 = (bf16[32,3584]{1,0:T(8,128)(2,1)S(1)}, bf16[32,3584]{1,0:T(8,128)(2,1)S(1)}, u32[]{:S(2)}, u32[]{:S(2)}) collective-permute-start(bf16[32,3584]{1,0:T(8,128)(2,1)S(1)} %slice.97), channel_id=1, source_target_pairs={{0,8},{1,25},{2,10},{3,27},{4,12},{5,29},{6,14},{7,31},{8,0},{9,17... | collective-permute-start | bytes 688136 | tf_op jit(solution)/shard_map/ppermute | solution.py:51
  55.5 7.3 %collective-permute-start.7 = (bf16[32,3584]{1,0:T(8,128)(2,1)S(1)}, bf16[32,3584]{1,0:T(8,128)(2,1)S(1)}, u32[]{:S(2)}, u32[]{:S(2)}) collective-permute-start(bf16[32,3584]{1,0:T(8,128)(2,1)S(1)} %slice.103), channel_id=1, source_target_pairs={{0,2},{1,7},{2,0},{3,5},{4,6},{5,3},{6,4},{7,1},{8,10},{9,15},{10,... | collective-permute-start | bytes 688136 | tf_op jit(solution)/shard_map/ppermute | solution.py:51
  62.9 6.1 %collective-permute-start.8 = (bf16[16,3584]{1,0:T(8,128)(2,1)S(1)}, bf16[16,3584]{1,0:T(8,128)(2,1)S(1)}, u32[]{:S(2)}, u32[]{:S(2)}) collective-permute-start(bf16[16,3584]{1,0:T(8,128)(2,1)S(1)} %slice.105), channel_id=1, source_target_pairs={{0,24},{1,9},{2,26},{3,11},{4,28},{5,13},{6,30},{7,15},{8,16},{9,1... | collective-permute-start | bytes 344072 | tf_op jit(solution)/shard_map/ppermute | solution.py:51
  73.7 6.7 %collective-permute-start.14 = (bf16[8,7296]{1,0:T(8,128)(2,1)S(1)}, bf16[8,7296]{1,0:T(8,128)(2,1)S(1)}, u32[]{:S(2)}, u32[]{:S(2)}) collective-permute-start(bf16[8,7296]{1,0:T(8,128)(2,1)S(1)} %pad_maximum_fusion.6), channel_id=1, source_target_pairs={{0,64},{1,65},{2,66},{3,67},{4,68},{5,69},{6,70},{7,71},{8,72},{9,... | collective-permute-start | bytes 350216 | tf_op jit(solution)/shard_map/ppermute | solution.py:55
  78.4 45.2 %collective-permute-start.19 = (bf16[1,7168,256]{2,1,0:T(8,128)(2,1)}, bf16[1,7168,256]{2,1,0:T(8,128)(2,1)}, u32[]{:S(2)}, u32[]{:S(2)}) collective-permute-start(bf16[1,7168,256]{2,1,0:T(8,128)(2,1)} %gate_own.7), channel_id=1, source_target_pairs={{0,1},{1,0},{2,3},{3,2},{4,5},{5,4},{6,7},{7,6},{8,9},{9,8},{10,11... | collective-permute-start | bytes 11010056 | tf_op jit(solution)/shard_map/ppermute | solution.py:59
  78.4 45.2 %collective-permute-start.20 = (bf16[1,7168,256]{2,1,0:T(8,128)(2,1)}, bf16[1,7168,256]{2,1,0:T(8,128)(2,1)}, u32[]{:S(2)}, u32[]{:S(2)}) collective-permute-start(bf16[1,7168,256]{2,1,0:T(8,128)(2,1)} %up_own.7), channel_id=1, source_target_pairs={{0,1},{1,0},{2,3},{3,2},{4,5},{5,4},{6,7},{7,6},{8,9},{9,8},{10,11... | collective-permute-start | bytes 11010056 | tf_op jit(solution)/shard_map/ppermute | solution.py:59
  78.9 44.6 %collective-permute-start.21 = (bf16[1,256,7168]{2,1,0:T(8,128)(2,1)}, bf16[1,256,7168]{2,1,0:T(8,128)(2,1)}, u32[]{:S(2)}, u32[]{:S(2)}) collective-permute-start(bf16[1,256,7168]{2,1,0:T(8,128)(2,1)} %down_own.7), channel_id=1, source_target_pairs={{0,1},{1,0},{2,3},{3,2},{4,5},{5,4},{6,7},{7,6},{8,9},{9,8},{10,11... | collective-permute-start | bytes 11010056 | tf_op jit(solution)/shard_map/ppermute | solution.py:59
  80.3 6.6 %collective-permute-start.10 = (bf16[8,7296]{1,0:T(8,128)(2,1)S(1)}, bf16[8,7296]{1,0:T(8,128)(2,1)S(1)}, u32[]{:S(2)}, u32[]{:S(2)}) collective-permute-start(bf16[8,7296]{1,0:T(8,128)(2,1)S(1)} %pad_maximum_fusion.6), channel_id=1, source_target_pairs={{0,32},{1,97},{2,34},{3,99},{4,36},{5,101},{6,38},{7,103},{8,40},{... | collective-permute-start | bytes 350216 | tf_op jit(solution)/shard_map/ppermute | solution.py:55
  83.3 6.9 %collective-permute-start.16 = (bf16[16,7296]{1,0:T(8,128)(2,1)S(1)}, bf16[16,7296]{1,0:T(8,128)(2,1)S(1)}, u32[]{:S(2)}, u32[]{:S(2)}) collective-permute-start(bf16[16,7296]{1,0:T(8,128)(2,1)S(1)} %pad_maximum_fusion.5), channel_id=1, source_target_pairs={{0,8},{1,25},{2,10},{3,27},{4,12},{5,29},{6,14},{7,31},{8,0},{9,17... | collective-permute-start | bytes 700424 | tf_op jit(solution)/shard_map/ppermute | solution.py:51
  87.0 6.6 %collective-permute-start.11 = (bf16[16,7296]{1,0:T(8,128)(2,1)S(1)}, bf16[16,7296]{1,0:T(8,128)(2,1)S(1)}, u32[]{:S(2)}, u32[]{:S(2)}) collective-permute-start(bf16[16,7296]{1,0:T(8,128)(2,1)S(1)} %pad_maximum_fusion.4), channel_id=1, source_target_pairs={{0,2},{1,7},{2,0},{3,5},{4,6},{5,3},{6,4},{7,1},{8,10},{9,15},{10,... | collective-permute-start | bytes 700424 | tf_op jit(solution)/shard_map/ppermute | solution.py:51
  90.2 9.9 %collective-permute-start.17 = (bf16[32,7296]{1,0:T(8,128)(2,1)S(1)}, bf16[32,7296]{1,0:T(8,128)(2,1)S(1)}, u32[]{:S(2)}, u32[]{:S(2)}) collective-permute-start(bf16[32,7296]{1,0:T(8,128)(2,1)S(1)} %pad_maximum_fusion.2), channel_id=1, source_target_pairs={{0,24},{1,9},{2,26},{3,11},{4,28},{5,13},{6,30},{7,15},{8,16},{9,1... | collective-permute-start | bytes 1400840 | tf_op jit(solution)/shard_map/ppermute | solution.py:51
  93.6 11.8 %collective-permute-start.12 = (bf16[32,7296]{1,0:T(8,128)(2,1)S(1)}, bf16[32,7296]{1,0:T(8,128)(2,1)S(1)}, u32[]{:S(2)}, u32[]{:S(2)}) collective-permute-start(bf16[32,7296]{1,0:T(8,128)(2,1)S(1)} %pad_maximum_fusion.1), channel_id=1, source_target_pairs={{0,6},{1,3},{2,4},{3,1},{4,2},{5,7},{6,0},{7,5},{8,14},{9,11},{10,... | collective-permute-start | bytes 1400840 | tf_op jit(solution)/shard_map/ppermute | solution.py:51
  100.1 14.8 %collective-permute-start.18 = (bf16[64,7296]{1,0:T(8,128)(2,1)S(1)}, bf16[64,7296]{1,0:T(8,128)(2,1)S(1)}, u32[]{:S(2)}, u32[]{:S(2)}) collective-permute-start(bf16[64,7296]{1,0:T(8,128)(2,1)S(1)} %constant_dynamic-update-slice_fusion.xb), channel_id=1, source_target_pairs={{0,2},{1,7},{2,4},{3,1},{4,6},{5,3},{6,0},{7,5},{8,10},{9,15},{10,... | collective-permute-start | bytes 2801672 | tf_op jit(solution)/shard_map/ppermute | solution.py:55
  105.5 14.2 %collective-permute-start.13 = (bf16[64,7296]{1,0:T(8,128)(2,1)S(1)}, bf16[64,7296]{1,0:T(8,128)(2,1)}, u32[]{:S(2)}, u32[]{:S(2)}) collective-permute-start(bf16[64,7296]{1,0:T(8,128)(2,1)S(1)} %pad_maximum_fusion.xa), channel_id=1, source_target_pairs={{0,8},{1,25},{2,10},{3,27},{4,12},{5,29},{6,14},{7,31},{8,16},{9,1... | collective-permute-start | bytes 2801672 | tf_op jit(solution)/shard_map/ppermute | solution.py:55
  115.0 31.2 %collective-permute-start.24 = (bf16[64,7296]{1,0:T(8,128)(2,1)S(1)}, bf16[64,7296]{1,0:T(8,128)(2,1)S(1)}, u32[]{:S(2)}, u32[]{:S(2)}) collective-permute-start(bf16[64,7296]{1,0:T(8,128)(2,1)S(1)} %collective-permute-done.18.xb), channel_id=1, source_target_pairs={{0,2},{1,7},{2,4},{3,1},{4,6},{5,3},{6,0},{7,5},{8,10},{9,15},{10,... | collective-permute-start | bytes 2801672 | tf_op jit(solution)/shard_map/ppermute | solution.py:55
  119.7 26.5 %collective-permute-start.23 = (bf16[64,7296]{1,0:T(8,128)(2,1)}, bf16[64,7296]{1,0:T(8,128)(2,1)S(1)}, u32[]{:S(2)}, u32[]{:S(2)}) collective-permute-start(bf16[64,7296]{1,0:T(8,128)(2,1)} %collective-permute-done.13.xa), channel_id=1, source_target_pairs={{0,8},{1,25},{2,10},{3,27},{4,12},{5,29},{6,14},{7,31},{8,16},{9,1... | collective-permute-start | bytes 2801672 | tf_op jit(solution)/shard_map/ppermute | solution.py:55
  133.6 22.8 %collective-permute-start.22 = (bf16[64,7168]{1,0:T(8,128)(2,1)S(1)}, bf16[64,7168]{1,0:T(8,128)(2,1)S(1)}, u32[]{:S(2)}, u32[]{:S(2)}) collective-permute-start(bf16[64,7168]{1,0:T(8,128)(2,1)S(1)} %get-tuple-element.21), channel_id=1, source_target_pairs={{0,8},{1,25},{2,10},{3,27},{4,12},{5,29},{6,14},{7,31},{8,16},{9,1... | collective-permute-start | bytes 2752520 | tf_op jit(solution)/shard_map/ppermute | solution.py:55
  143.9 15.1 %collective-permute-start.32 = (bf16[64,7168]{1,0:T(8,128)(2,1)S(1)}, bf16[64,7168]{1,0:T(8,128)(2,1)S(1)}, u32[]{:S(2)}, u32[]{:S(2)}) collective-permute-start(bf16[64,7168]{1,0:T(8,128)(2,1)S(1)} %get-tuple-element.25), channel_id=1, source_target_pairs={{0,2},{1,7},{2,4},{3,1},{4,6},{5,3},{6,0},{7,5},{8,10},{9,15},{10,... | collective-permute-start | bytes 2752520 | tf_op jit(solution)/shard_map/ppermute | solution.py:55
  156.6 33.7 %collective-permute-start.25 = (bf16[64,7168]{1,0:T(8,128)(2,1)S(1)}, bf16[64,7168]{1,0:T(8,128)(2,1)S(1)}, u32[]{:S(2)}, u32[]{:S(2)}) collective-permute-start(bf16[64,7168]{1,0:T(8,128)(2,1)S(1)} %add_convert_fusion.5), channel_id=1, source_target_pairs={{0,8},{1,25},{2,10},{3,27},{4,12},{5,29},{6,14},{7,31},{8,16},{9,1... | collective-permute-start | bytes 2752520 | tf_op jit(solution)/shard_map/ppermute | solution.py:55
  156.7 14.8 %collective-permute-start.27 = (bf16[64,7296]{1,0:T(8,128)(2,1)S(1)}, bf16[64,7296]{1,0:T(8,128)(2,1)S(1)}, u32[]{:S(2)}, u32[]{:S(2)}) collective-permute-start(bf16[64,7296]{1,0:T(8,128)(2,1)S(1)} %collective-permute-done.24.xb), channel_id=1, source_target_pairs={{0,2},{1,7},{2,4},{3,1},{4,6},{5,3},{6,0},{7,5},{8,10},{9,15},{10,... | collective-permute-start | bytes 2801672 | tf_op jit(solution)/shard_map/ppermute | solution.py:55
  156.8 23.3 %collective-permute-start.26 = (bf16[64,7296]{1,0:T(8,128)(2,1)S(1)}, bf16[64,7296]{1,0:T(8,128)(2,1)S(1)}, u32[]{:S(2)}, u32[]{:S(2)}) collective-permute-start(bf16[64,7296]{1,0:T(8,128)(2,1)S(1)} %collective-permute-done.23.xa), channel_id=1, source_target_pairs={{0,8},{1,25},{2,10},{3,27},{4,12},{5,29},{6,14},{7,31},{8,16},{9,1... | collective-permute-start | bytes 2801672 | tf_op jit(solution)/shard_map/ppermute | solution.py:55
  159.3 32.5 %collective-permute-start.33 = (bf16[64,7168]{1,0:T(8,128)(2,1)S(1)}, bf16[64,7168]{1,0:T(8,128)(2,1)S(1)}, u32[]{:S(2)}, u32[]{:S(2)}) collective-permute-start(bf16[64,7168]{1,0:T(8,128)(2,1)S(1)} %add_convert_fusion.2), channel_id=1, source_target_pairs={{0,2},{1,7},{2,4},{3,1},{4,6},{5,3},{6,0},{7,5},{8,10},{9,15},{10,... | collective-permute-start | bytes 2752520 | tf_op jit(solution)/shard_map/ppermute | solution.py:55
  190.5 18.4 %collective-permute-start.28 = (bf16[64,7168]{1,0:T(8,128)(2,1)S(1)}, bf16[64,7168]{1,0:T(8,128)(2,1)S(1)}, u32[]{:S(2)}, u32[]{:S(2)}) collective-permute-start(bf16[64,7168]{1,0:T(8,128)(2,1)S(1)} %add_convert_fusion.4), channel_id=1, source_target_pairs={{0,8},{1,25},{2,10},{3,27},{4,12},{5,29},{6,14},{7,31},{8,16},{9,1... | collective-permute-start | bytes 2752520 | tf_op jit(solution)/shard_map/ppermute | solution.py:55
  192.0 18.8 %collective-permute-start.34 = (bf16[64,7168]{1,0:T(8,128)(2,1)S(1)}, bf16[64,7168]{1,0:T(8,128)(2,1)S(1)}, u32[]{:S(2)}, u32[]{:S(2)}) collective-permute-start(bf16[64,7168]{1,0:T(8,128)(2,1)S(1)} %add_convert_fusion.1), channel_id=1, source_target_pairs={{0,2},{1,7},{2,4},{3,1},{4,6},{5,3},{6,0},{7,5},{8,10},{9,15},{10,... | collective-permute-start | bytes 2752520 | tf_op jit(solution)/shard_map/ppermute | solution.py:55
  209.2 9.8 %collective-permute-start.29 = (bf16[32,7168]{1,0:T(8,128)(2,1)S(1)}, bf16[32,7168]{1,0:T(8,128)(2,1)S(1)}, u32[]{:S(2)}, u32[]{:S(2)}) collective-permute-start(bf16[32,7168]{1,0:T(8,128)(2,1)S(1)} %slice.109), channel_id=1, source_target_pairs={{0,6},{1,3},{2,4},{3,1},{4,2},{5,7},{6,0},{7,5},{8,14},{9,11},{10,... | collective-permute-start | bytes 1376264 | tf_op jit(solution)/shard_map/ppermute | solution.py:51
  211.1 9.8 %collective-permute-start.35 = (bf16[32,7168]{1,0:T(8,128)(2,1)S(1)}, bf16[32,7168]{1,0:T(8,128)(2,1)S(1)}, u32[]{:S(2)}, u32[]{:S(2)}) collective-permute-start(bf16[32,7168]{1,0:T(8,128)(2,1)S(1)} %slice.115), channel_id=1, source_target_pairs={{0,24},{1,9},{2,26},{3,11},{4,28},{5,13},{6,30},{7,15},{8,16},{9,1... | collective-permute-start | bytes 1376264 | tf_op jit(solution)/shard_map/ppermute | solution.py:51
  227.2 6.4 %collective-permute-start.37 = (bf16[8,7168]{1,0:T(8,128)(2,1)S(1)}, bf16[8,7168]{1,0:T(8,128)(2,1)S(1)}, u32[]{:S(2)}, u32[]{:S(2)}) collective-permute-start(bf16[8,7168]{1,0:T(8,128)(2,1)S(1)} %get-tuple-element.31), channel_id=1, source_target_pairs={{0,64},{1,65},{2,66},{3,67},{4,68},{5,69},{6,70},{7,71},{8,72},{9,... | collective-permute-start | bytes 344072 | tf_op jit(solution)/shard_map/ppermute | solution.py:55
  (13 other events, 102.7 us)
